TPU v7x, 32 devices: a whole 2x2x4 slice. The times are simulated.
32 devices in a mesh: expert: 8 (over y, x, core), tensor: 4 (over z).
Axes of the slice: x: 2, y: 2, z: 4, core: 2. Of those that a mesh axis runs over, the one named last changes fastest.
Arguments:
- tokens: bfloat16 [8192, 1024], P('expert'), may hold values from -6 to 6
- cotangent: bfloat16 [8192, 1024], P('expert'), may hold values from -6 to 6
- routes: int32 [8192], P('expert'), may hold values from 0 to 15, as said below
- slot_index: int32 [8192], P('expert'), may hold values from 0 to 128, as said below
- first_gain: float32 [1024], replicated, may hold values from 0.1 to 1.9
- first_shift: float32 [1024], replicated, may hold values from -1.25 to 1.25
- project_in: bfloat16 [1024, 3, 1024], P(None, None, 'tensor'), may hold values from -0.25 to 0.25
- project_out: bfloat16 [1024, 1024], P('tensor'), may hold values from -1.5 to 1.5
- second_gain: float32 [1024], replicated, may hold values from 0.1 to 1.9
- second_shift: float32 [1024], replicated, may hold values from -1.25 to 1.25
- router_weight: bfloat16 [1024, 16], replicated, may hold values from -0.09375 to 0.09375
- mixing_weight: bfloat16 [1024, 2], replicated, may hold values from -0.1875 to 0.1875
- dense_up: bfloat16 [1024, 4096], P(None, 'tensor'), may hold values from -0.1875 to 0.1875
- dense_down: bfloat16 [4096, 1024], P('tensor'), may hold values from -0.1875 to 0.1875
- expert_up: bfloat16 [16, 1024, 4096], P('expert', None, 'tensor'), may hold values from -0.375 to 0.375
- expert_down: bfloat16 [16, 4096, 1024], P('expert', 'tensor'), may hold values from -3 to 3
Outputs:
- layer_out: bfloat16 [8192, 1024], P('expert')
- input_grad: bfloat16 [8192, 1024], P('expert')
- first_gain_grad: float32 [1024], replicated
- first_shift_grad: float32 [1024], replicated
- project_in_grad: float32 [1024, 3, 1024], P(None, None, 'tensor')
- project_out_grad: float32 [1024, 1024], P('tensor')
- second_gain_grad: float32 [1024], replicated
- second_shift_grad: float32 [1024], replicated
- router_grad: float32 [1024, 16], replicated
- mixing_grad: float32 [1024, 2], replicated
- dense_up_grad: float32 [1024, 4096], P(None, 'tensor')
- dense_down_grad: float32 [4096, 1024], P('tensor')
- expert_up_grad: float32 [16, 1024, 4096], P('expert', None, 'tensor')
- expert_down_grad: float32 [16, 4096, 1024], P('expert', 'tensor')
Inputs may be any that keep to these rules, and one draw needn't show every extreme that they name: `routes`: in every block of 1024 tokens (tokens b * 1024 to (b + 1) * 1024 - 1) some expert is named by more than 128 tokens. slot_index[t] is the number of earlier tokens of t's block with the same route, or 128 where that number is 128 or more (the token is dropped); so at most 128 kept tokens of a block name one expert, and every block fills all 128 slots of some expert.
All inputs are finite; a program needn't handle non-finite values.
Results may differ from a plain program's by a relative error of at most 0.023.
Values may be sent and summed in bfloat16 or wider, within the bound.
No kernel may reach another device: no remote copies, remote signals or barrier semaphores. Data moves between devices by JAX's collectives and lax.ppermute only.
A program may use at most 192 MiB of HBM per device.

v0:
```python
import jax
import jax.numpy as jnp
from jax import lax
from jax.sharding import PartitionSpec as P

HEAD_DIM = 64
SEQ = 1024
EPS = 1e-05
NEGATIVE = -1e30


def layer_norm(row_values, norm_gain, norm_shift):
    row_mean = jnp.mean(row_values, axis=-1, keepdims=True)
    centred = row_values - row_mean
    spread = jnp.mean(centred * centred, axis=-1, keepdims=True)
    return centred * lax.rsqrt(spread + EPS) * norm_gain + norm_shift


def gelu_tanh(values):
    return jax.nn.gelu(values, approximate=True)


def gelu_back(pre_act, incoming):
    return jax.vjp(gelu_tanh, pre_act)[1](incoming)[0]


def causal_scores(query_block, key_seq, offset):
    score_scale = HEAD_DIM ** (-0.5)
    scores = (
        jnp.einsum("qhd,khd->hqk", query_block, key_seq, preferred_element_type=jnp.float32)
        * score_scale
    )
    query_pos = offset + lax.iota(jnp.int32, query_block.shape[0])
    key_pos = lax.iota(jnp.int32, key_seq.shape[0])
    allowed = key_pos[None, :] <= query_pos[:, None]
    return jnp.where(allowed[None], scores, NEGATIVE)


def attend_forward(queries, key_rows, values, block_rows):
    row_count, head_count, head_width = queries.shape
    per_seq = SEQ // block_rows

    def one_block(block_index):
        seq_start = block_index // per_seq * SEQ
        offset = block_index % per_seq * block_rows
        query_block = lax.dynamic_slice_in_dim(queries, seq_start + offset, block_rows, 0)
        scores = causal_scores(query_block, key_rows, offset)
        row_max = jnp.max(scores, axis=-1, keepdims=True)
        powers = jnp.exp(scores - row_max)
        row_total = jnp.sum(powers, axis=-1, keepdims=True)
        weights = (powers / row_total).astype(jnp.bfloat16)
        blended = jnp.einsum("hqk,khd->qhd", weights, values, preferred_element_type=jnp.float32)
        return (blended.astype(jnp.bfloat16), (row_max + jnp.log(row_total))[..., 0])

    blended, log_total = lax.map(one_block, jnp.arange(row_count // block_rows, dtype=jnp.int32))
    return (blended.reshape(row_count, head_count * head_width), log_total)


def attend_backward(queries, key_rows, values, log_total, grad_blended, block_rows):
    row_count, head_count, head_width = queries.shape
    per_seq = SEQ // block_rows
    score_scale = HEAD_DIM ** (-0.5)

    def one_seq(sequence):
        seq_start = sequence * SEQ

        def step(totals, inner_index):
            key_acc, value_acc = totals
            offset = inner_index * block_rows
            query_block = lax.dynamic_slice_in_dim(queries, seq_start + offset, block_rows, 0)
            grad_block = lax.dynamic_slice_in_dim(grad_blended, seq_start + offset, block_rows, 0)
            row_log = lax.dynamic_index_in_dim(
                log_total, sequence * per_seq + inner_index, 0, keepdims=False
            )
            scores = causal_scores(query_block, key_rows, offset)
            weights = jnp.exp(scores - row_log[..., None])
            weight_grad = jnp.einsum(
                "qhd,khd->hqk", grad_block, values, preferred_element_type=jnp.float32
            )
            row_inner = jnp.sum(weights * weight_grad, axis=-1, keepdims=True)
            score_grad = (weights * (weight_grad - row_inner)).astype(jnp.bfloat16)
            query_grad = (
                jnp.einsum("hqk,khd->qhd", score_grad, key_rows, preferred_element_type=jnp.float32)
                * score_scale
            )
            key_acc = (
                key_acc
                + jnp.einsum(
                    "hqk,qhd->khd", score_grad, query_block, preferred_element_type=jnp.float32
                )
                * score_scale
            )
            value_acc = value_acc + jnp.einsum(
                "hqk,qhd->khd",
                weights.astype(jnp.bfloat16),
                grad_block,
                preferred_element_type=jnp.float32,
            )
            return ((key_acc, value_acc), query_grad)

        empty_acc = jnp.zeros((SEQ, head_count, head_width), jnp.float32)
        (key_grad, value_grad), query_grad = lax.scan(
            step, (empty_acc, empty_acc), jnp.arange(per_seq, dtype=jnp.int32)
        )
        return (query_grad.reshape(SEQ, head_count, head_width), key_grad, value_grad)

    query_grad, key_grad, value_grad = lax.map(
        one_seq, jnp.arange(row_count // SEQ, dtype=jnp.int32)
    )
    flat_width = head_count * head_width
    return jnp.stack(
        [
            query_grad.reshape(row_count, flat_width),
            key_grad.reshape(row_count, flat_width),
            value_grad.reshape(row_count, flat_width),
        ],
        axis=1,
    )


def send_home(buffer):
    return lax.all_to_all(
        buffer.astype(jnp.bfloat16), "expert", split_axis=1, concat_axis=0, tiled=True
    ).astype(buffer.dtype)


def send_grads_home(buffer):
    return lax.all_to_all(
        buffer.astype(jnp.bfloat16), "expert", split_axis=1, concat_axis=0, tiled=True
    ).astype(buffer.dtype)


def local(
    tokens,
    cotangent,
    routes,
    slot_index,
    first_gain,
    first_shift,
    project_in,
    project_out,
    second_gain,
    second_shift,
    router_weight,
    mixing_weight,
    dense_up,
    dense_down,
    expert_up,
    expert_down,
):
    inputs = tokens.astype(jnp.float32)
    cotan_rows = cotangent.astype(jnp.float32)
    row_count, model_width = inputs.shape
    expert_count = router_weight.shape[1]
    capacity = 2 * row_count // expert_count
    head_count = project_in.shape[2] // HEAD_DIM
    block_rows = min(512, SEQ)
    normed_in, first_back = jax.vjp(layer_norm, inputs, first_gain, first_shift)
    normed_low = normed_in.astype(jnp.bfloat16)
    projected = jnp.einsum(
        "td,dcn->tcn", normed_low, project_in, preferred_element_type=jnp.float32
    ).astype(jnp.bfloat16)
    queries = projected[:, 0].reshape(row_count, head_count, HEAD_DIM)
    key_rows = projected[:, 1].reshape(row_count, head_count, HEAD_DIM)
    values = projected[:, 2].reshape(row_count, head_count, HEAD_DIM)
    attended, log_total = attend_forward(queries, key_rows, values, block_rows)
    attn_part = jnp.dot(attended, project_out, preferred_element_type=jnp.float32)
    attn_full = lax.psum(attn_part, "tensor")
    residual = inputs + attn_full
    normed_mid, second_back = jax.vjp(layer_norm, residual, second_gain, second_shift)
    mid_low = normed_mid.astype(jnp.bfloat16)
    router_logits = jnp.dot(mid_low, router_weight, preferred_element_type=jnp.float32)
    mixing_logits = jnp.dot(mid_low, mixing_weight, preferred_element_type=jnp.float32)
    chosen = routes[:, None] == lax.iota(jnp.int32, expert_count)[None, :]

    def gating(route_logits, mix_logits):
        router_probs = jax.nn.softmax(route_logits, axis=-1)
        return (
            jnp.sum(jnp.where(chosen, router_probs, 0.0), axis=-1),
            jax.nn.softmax(mix_logits, axis=-1),
        )

    (gate_value, mixing), gating_back = jax.vjp(gating, router_logits, mixing_logits)
    slot_total = expert_count * capacity
    slot_place = jnp.where(slot_index < capacity, routes * capacity + slot_index, slot_total)
    holder = (
        jnp.full((slot_total,), row_count, jnp.int32)
        .at[slot_place]
        .set(lax.iota(jnp.int32, row_count), mode="drop")
    )

    def to_slots(row_values):
        taken = jnp.take(row_values, holder, axis=0, mode="fill", fill_value=0)
        return taken.reshape(expert_count, capacity, row_values.shape[1])

    def from_slots(buffer):
        return jnp.take(
            buffer.reshape(slot_total, buffer.shape[-1]),
            slot_place,
            axis=0,
            mode="fill",
            fill_value=0,
        )

    arrived = lax.all_to_all(to_slots(mid_low), "expert", split_axis=0, concat_axis=1, tiled=True)
    expert_pre = jnp.einsum("erd,edf->erf", arrived, expert_up, preferred_element_type=jnp.float32)
    expert_hidden = gelu_tanh(expert_pre).astype(jnp.bfloat16)
    expert_part = jnp.einsum(
        "erf,efd->erd", expert_hidden, expert_down, preferred_element_type=jnp.float32
    )
    dense_pre = jnp.dot(mid_low, dense_up, preferred_element_type=jnp.float32)
    dense_hidden = gelu_tanh(dense_pre).astype(jnp.bfloat16)
    dense_part = jnp.dot(dense_hidden, dense_down, preferred_element_type=jnp.float32)
    dense_weight = mixing[:, 0:1]
    expert_weight = (mixing[:, 1] * gate_value)[:, None]
    dense_full, expert_full = (
        lax.psum(dense_part.astype(jnp.bfloat16), "tensor").astype(jnp.float32),
        lax.psum(expert_part.astype(jnp.bfloat16), "tensor").astype(jnp.float32),
    )
    expert_tok = from_slots(send_home(expert_full))
    layer_out = residual + dense_weight * dense_full + expert_weight * expert_tok
    dense_dot = jnp.sum(cotan_rows * dense_full, axis=-1)
    expert_dot = jnp.sum(cotan_rows * expert_tok, axis=-1)
    dense_out_grad = (cotan_rows * dense_weight).astype(jnp.bfloat16)
    expert_tok_grad = (cotan_rows * expert_weight).astype(jnp.bfloat16)
    mixing_dots = jnp.stack([dense_dot, gate_value * expert_dot], axis=-1)
    gate_grad = mixing[:, 1] * expert_dot
    router_logit_grad, mixing_logit_grad = gating_back((gate_grad, mixing_dots))
    router_low = router_logit_grad.astype(jnp.bfloat16)
    mixing_low = mixing_logit_grad.astype(jnp.bfloat16)
    router_grad = jnp.einsum("td,te->de", mid_low, router_low, preferred_element_type=jnp.float32)
    mixing_grad = jnp.einsum("td,te->de", mid_low, mixing_low, preferred_element_type=jnp.float32)
    mid_from_gates = jnp.einsum(
        "te,de->td", router_low, router_weight, preferred_element_type=jnp.float32
    ) + jnp.einsum("te,de->td", mixing_low, mixing_weight, preferred_element_type=jnp.float32)
    dense_down_grad = jnp.einsum(
        "tf,td->fd", dense_hidden, dense_out_grad, preferred_element_type=jnp.float32
    )
    dense_hidden_grad = jnp.einsum(
        "td,fd->tf", dense_out_grad, dense_down, preferred_element_type=jnp.float32
    )
    dense_pre_grad = gelu_back(dense_pre, dense_hidden_grad).astype(jnp.bfloat16)
    dense_up_grad = jnp.einsum(
        "td,tf->df", mid_low, dense_pre_grad, preferred_element_type=jnp.float32
    )
    mid_dense_part = jnp.einsum(
        "tf,df->td", dense_pre_grad, dense_up, preferred_element_type=jnp.float32
    )
    grad_arrived = lax.all_to_all(
        to_slots(expert_tok_grad), "expert", split_axis=0, concat_axis=1, tiled=True
    )
    expert_down_grad = jnp.einsum(
        "erf,erd->efd", expert_hidden, grad_arrived, preferred_element_type=jnp.float32
    )
    expert_hidden_grad = jnp.einsum(
        "erd,efd->erf", grad_arrived, expert_down, preferred_element_type=jnp.float32
    )
    expert_pre_grad = gelu_back(expert_pre, expert_hidden_grad).astype(jnp.bfloat16)
    expert_up_grad = jnp.einsum(
        "erd,erf->edf", arrived, expert_pre_grad, preferred_element_type=jnp.float32
    )
    arrived_grad = jnp.einsum(
        "erf,edf->erd", expert_pre_grad, expert_up, preferred_element_type=jnp.float32
    )
    mid_dense, arrived_full = (
        lax.psum(mid_dense_part.astype(jnp.bfloat16), "tensor").astype(jnp.float32),
        lax.psum(arrived_grad.astype(jnp.bfloat16), "tensor").astype(jnp.float32),
    )
    mid_grad = mid_dense + from_slots(send_grads_home(arrived_full)) + mid_from_gates
    resid_from_mid, second_gain_grad, second_shift_grad = second_back(mid_grad)
    residual_grad = cotan_rows + resid_from_mid
    attn_grad_low = residual_grad.astype(jnp.bfloat16)
    project_out_grad = jnp.einsum(
        "tn,td->nd", attended, attn_grad_low, preferred_element_type=jnp.float32
    )
    attended_grad = jnp.einsum(
        "td,nd->tn", attn_grad_low, project_out, preferred_element_type=jnp.float32
    ).astype(jnp.bfloat16)
    qkv_grad = attend_backward(
        queries,
        key_rows,
        values,
        log_total,
        attended_grad.reshape(row_count, head_count, HEAD_DIM),
        block_rows,
    ).astype(jnp.bfloat16)
    project_in_grad = jnp.einsum(
        "td,tcn->dcn", normed_low, qkv_grad, preferred_element_type=jnp.float32
    )
    normed_part = jnp.einsum(
        "tcn,dcn->td", qkv_grad, project_in, preferred_element_type=jnp.float32
    )
    normed_grad = lax.psum(normed_part.astype(jnp.bfloat16), "tensor").astype(jnp.float32)
    input_from_norm, first_gain_grad, first_shift_grad = first_back(normed_grad)
    input_grad = (residual_grad + input_from_norm).astype(jnp.bfloat16)
    (
        router_grad,
        mixing_grad,
        dense_up_grad,
        dense_down_grad,
        second_gain_grad,
        second_shift_grad,
        project_out_grad,
        project_in_grad,
        first_gain_grad,
        first_shift_grad,
    ) = (
        lax.psum(router_grad.astype(jnp.bfloat16), "expert").astype(jnp.float32),
        lax.psum(mixing_grad.astype(jnp.bfloat16), "expert").astype(jnp.float32),
        lax.psum(dense_up_grad.astype(jnp.bfloat16), "expert").astype(jnp.float32),
        lax.psum(dense_down_grad.astype(jnp.bfloat16), "expert").astype(jnp.float32),
        lax.psum(second_gain_grad.astype(jnp.bfloat16), "expert").astype(jnp.float32),
        lax.psum(second_shift_grad.astype(jnp.bfloat16), "expert").astype(jnp.float32),
        lax.psum(project_out_grad.astype(jnp.bfloat16), "expert").astype(jnp.float32),
        lax.psum(project_in_grad.astype(jnp.bfloat16), "expert").astype(jnp.float32),
        lax.psum(first_gain_grad.astype(jnp.bfloat16), "expert").astype(jnp.float32),
        lax.psum(first_shift_grad.astype(jnp.bfloat16), "expert").astype(jnp.float32),
    )
    return (
        layer_out.astype(jnp.bfloat16),
        input_grad,
        first_gain_grad,
        first_shift_grad,
        project_in_grad,
        project_out_grad,
        second_gain_grad,
        second_shift_grad,
        router_grad,
        mixing_grad,
        dense_up_grad,
        dense_down_grad,
        expert_up_grad,
        expert_down_grad,
    )


def solution(mesh):
    placed = (
        P("expert", None),
        P("expert", None),
        P("expert"),
        P("expert"),
        P(),
        P(),
        P(None, None, "tensor"),
        P("tensor", None),
        P(),
        P(),
        P(),
        P(),
        P(None, "tensor"),
        P("tensor", None),
        P("expert", None, "tensor"),
        P("expert", "tensor", None),
    )
    return jax.shard_map(
        local,
        mesh=mesh,
        in_specs=placed,
        out_specs=(
            P("expert", None),
            P("expert", None),
            P(),
            P(),
            P(None, None, "tensor"),
            P("tensor", None),
            P(),
            P(),
            P(),
            P(),
            P(None, "tensor"),
            P("tensor", None),
            P("expert", None, "tensor"),
            P("expert", "tensor", None),
        ),
        check_vma=False,
    )
```

profile of v0, /device:TPU:0, one launch (start us, length us, event | category | flops | bytes accessed | tf_op | source)
XLA Modules:
  0.0 1272.1 jit_solution(15387023293925295045)
XLA Ops:
  16.1 23.0 %while.43 = (s32[]{:T(128)}, bf16[2,512,4,64]{1,3,2,0:T(8,128)(2,1)}, f32[2,4,512]{2,1,0:T(4,128)S(1)}, s32[2]{0:T(128)S(1)}, bf16[1024,4,64]{0,2,1:T(8,128)(2,1...) while((s32[]{:T(128)}, ...), condition=%wide.region_5.6_spmd, body=%wide.region_2.5_spmd.sunk | while | flops 562690560 | bytes 35197428 | solution.py:55
  50.9 152.7 %all-reduce.10.cloned.1.call-done = f32[1024,1024]{1,0:T(8,128)} async-done(((f32[1024,1024]{1,0:T(8,128)}), f32[1024,1024]{1,0:T(8,128)}) %all-reduce.10.cloned.1.call-update) | async-done | bytes 4194320 | tf_op jit(solution)/shard_map/psum | solution.py:168
  211.6 12.8 %gather_fusion = bf16[2048,1024]{1,0:T(8,128)(2,1)} fusion(bf16[1024,1024]{1,0:T(8,128)(2,1)} %add_convert_fusion.1, s32[2048]{0:T(1024)S(1)} %fusion.86), kind=kCustom, calls=%fused_computation.clone | custom fusion | bytes 8396800 | tf_op jit(solution)/shard_map/jit(_take)/gather | solution.py:193
  243.4 38.5 %all-to-all-done = bf16[16,128,1024]{2,1,0:T(8,128)(2,1)} async-done(((bf16[16,128,1024]{2,1,0:T(8,128)(2,1)}), bf16[16,128,1024]{2,1,0:T(8,128)(2,1)}, u32[]{:S(2)}, u32[]{:S(2)}) %all-to-all-start) | async-done | bytes 4194336 | tf_op jit(solution)/shard_map/all_to_all | solution.py:205
  301.4 220.2 %all-reduce.18.cloned.1.call-done = (bf16[1024,1024]{1,0:T(8,128)(2,1)}, bf16[2,1024,1024]{2,1,0:T(8,128)(2,1)}) async-done(((bf16[1024,1024]{1,0:T(8,128)(2,1)}, bf16[2,1024,1024]{2,1,0:T(8,128)(2,1)}), (bf16[1024,1024]{1,0:T(8,128)(2,1)}, bf16[2,1024,1024]{2,1,0:T(8,128)(2,1)})) %all-reduce.18.cloned.1.call-update) | async-done | bytes 6291472 | tf_op jit(solution)/shard_map/psum | solution.py:217
  521.6 8.5 copy.55
  539.6 44.4 %all-to-all-done.1 = bf16[2,1024,1024]{2,0,1:T(2,128)(2,1)} async-done(((bf16[2,1024,1024]{2,0,1:T(2,128)(2,1)}), bf16[2,1024,1024]{2,0,1:T(2,128)(2,1)}, u32[]{:S(2)}, u32[]{:S(2)}) %all-to-all-start.1) | async-done | bytes 4194336 | tf_op jit(solution)/shard_map/all_to_all | solution.py:122
  584.0 7.1 copy.56
  591.1 9.7 gather_fusion.1
  607.2 12.8 %gather_fusion.2 = bf16[2048,1024]{1,0:T(8,128)(2,1)} fusion(bf16[1024,1024]{1,0:T(8,128)(2,1)} %fusion.66, s32[2048]{0:T(1024)S(1)} %fusion.86), kind=kCustom, calls=%fused_computation.2.clone | custom fusion | bytes 8396800 | tf_op jit(solution)/shard_map/jit(_take)/gather | solution.py:193
  628.5 7.7 fusion.62
  641.3 36.3 %all-to-all-done.2 = bf16[16,128,1024]{2,1,0:T(8,128)(2,1)} async-done(((bf16[16,128,1024]{2,1,0:T(8,128)(2,1)}), bf16[16,128,1024]{2,1,0:T(8,128)(2,1)}, u32[]{:S(2)}, u32[]{:S(2)}) %all-to-all-start.2) | async-done | bytes 4194336 | tf_op jit(solution)/shard_map/all_to_all | solution.py:249
  681.0 12.1 fusion.43
  701.3 220.1 %all-reduce.16.cloned.1.call-done = (bf16[2,1024,1024]{2,1,0:T(8,128)(2,1)}, bf16[1024,1024]{1,0:T(8,128)(2,1)}) async-done(((bf16[2,1024,1024]{2,1,0:T(8,128)(2,1)}, bf16[1024,1024]{1,0:T(8,128)(2,1)}), (bf16[2,1024,1024]{2,1,0:T(8,128)(2,1)}, bf16[1024,1024]{1,0:T(8,128)(2,1)})) %all-reduce.16.cloned.1.call-update) | async-done | bytes 6291472 | tf_op jit(solution)/shard_map/psum | solution.py:267
  921.5 8.5 copy.58
  939.6 44.2 %all-to-all-done.3 = bf16[2,1024,1024]{2,0,1:T(2,128)(2,1)} async-done(((bf16[2,1024,1024]{2,0,1:T(2,128)(2,1)}), bf16[2,1024,1024]{2,0,1:T(2,128)(2,1)}, u32[]{:S(2)}, u32[]{:S(2)}) %all-to-all-start.3) | async-done | bytes 4194336 | tf_op jit(solution)/shard_map/all_to_all | solution.py:128
  983.8 7.1 copy.59
  990.9 9.8 gather_fusion.3
  1000.8 7.5 multiply_reduce_fusion.1
  1016.7 33.2 %while.44 = (s32[]{:T(128)}, f32[1024,4,64]{0,2,1:T(8,128)}, f32[1024,4,64]{0,2,1:T(8,128)}, bf16[2,512,4,64]{1,3,2,0:T(8,128)(2,1)}, s32[2]{0:T(128)S(1)}, /*in...) while((s32[]{:T(128)}, f32[1024,4,64]{0,2,1:T(8,128)}, ...), condition=%wide.region_27.30_spmd.clone, body=%wide.region_25.29_spmd.clone.sunk | while | flops 1375599104 | bytes 97579512 | solution.py:102
  1077.9 13.6 %fusion.97 = f32[2,1024,1024]{2,1,0:T(8,128)} fusion(bf16[2,1024,1024]{2,1,0:T(8,128)(2,1)} %bitcast.152, f32[2,1024,1024]{2,1,0:T(8,128)} %copy-done.81), kind=kOutput, calls=%fused_computation.170 | convolution fusion | flops 4313841664 | bytes 20971520 | tf_op jit(solution)/shard_map/erf,erd->efd/dot_general | solution.py:252
  1098.4 47.4 %all-reduce.12.cloned.1.call-done = bf16[1024,1024]{1,0:T(8,128)(2,1)} async-done(((bf16[1024,1024]{1,0:T(8,128)(2,1)}), bf16[1024,1024]{1,0:T(8,128)(2,1)}) %all-reduce.12.cloned.1.call-update) | async-done | bytes 2097168 | tf_op jit(solution)/shard_map/psum | solution.py:293
  1153.4 26.6 %all-reduce = (bf16[1024]{0:T(1024)(128)(2,1)S(1)}, bf16[1024]{0:T(1024)(128)(2,1)S(1)}, bf16[1024]{0:T(1024)(128)(2,1)S(1)}, bf16[1024]{0:T(1024)(128)(2,1)S(1)...) all-reduce(bf16[1024]{0:T(1024)(128)(2,1)S(1)} %get-tuple-element.3, ...), channel_id=1, replica_groups=mesh['expert'=8,'tensor'=4] {'expert'}, use_global_device_ids=true, to_apply=%region_32.35 | all-reduce | flops 22528 | bytes 90112 | tf_op jit(solution)/shard_map/psum | solution.py:316
  1189.1 65.5 %all-reduce.14.cloned.1.call-done = (bf16[1024,3,256]{2,0,1:T(8,128)(2,1)}, bf16[256,1024]{1,0:T(8,128)(2,1)}, bf16[1024,1024]{1,0:T(8,128)(2,1)}, bf16[1024,1024]{1,0:T(8,128)(2,1)}) async-done(((bf16[1024,3,256]{2,0,1:T(8,128)(2,1)}, bf16[256,1024]{1,0:T(8,128)(2,1)}, bf16[1024,1024]{1,0:T(8,128)(2,1)}, bf16[1024,1024]{1,0:T(8,128)(2,1)}), (bf16[1024,3,256]{2,0,1:T(8,128)(2,1)}, ...) | async-done | bytes 6291472 | tf_op jit(solution)/shard_map/psum | solution.py:315
  (329 shorter events, 233.0 us)
Async XLA Ops:
  7.2 232.2 %copy-start = (bf16[1024,1024]{1,0:T(8,128)(2,1)S(1)}, bf16[1024,1024]{1,0:T(8,128)(2,1)}, u32[]{:S(2)}) copy-start(bf16[1024,1024]{1,0:T(8,128)(2,1)} %param.37) | copy-start | bytes 6291460
  7.2 196.4 %all-reduce.10.cloned.1.call-start = ((), (), s32[]{:S(2)}) async-start(), calls=%async_computation.4 | async-start | bytes 8388608 | tf_op jit(solution)/shard_map/psum | solution.py:168
  207.6 16.8 %copy-start.63 = (f32[1024]{0:T(1024)}, f32[1024]{0:T(1024)S(1)}, u32[]{:S(2)}) copy-start(f32[1024]{0:T(1024)S(1)} %multiply_reduce_fusion.3) | copy-start | bytes 12292
  228.2 53.7 %all-to-all-start = ((bf16[16,128,1024]{2,1,0:T(8,128)(2,1)}), bf16[16,128,1024]{2,1,0:T(8,128)(2,1)}, u32[]{:S(2)}, u32[]{:S(2)}) async-start(bf16[16,128,1024]{2,1,0:T(8,128)(2,1)} %bitcast.148), calls=%async_computation | async-start | bytes 8388608 | tf_op jit(solution)/shard_map/all_to_all | solution.py:205
  232.8 288.9 %all-reduce.18.cloned.1.call-start = ((), (), s32[]{:S(2)}) async-start(), calls=%async_computation.8 | async-start | bytes 12582912 | tf_op jit(solution)/shard_map/psum | solution.py:217
  286.7 7.9 copy-start.71
  530.2 53.8 %all-to-all-start.1 = ((bf16[2,1024,1024]{2,0,1:T(2,128)(2,1)}), bf16[2,1024,1024]{2,0,1:T(2,128)(2,1)}, u32[]{:S(2)}, u32[]{:S(2)}) async-start(bf16[2,1024,1024]{2,0,1:T(2,128)(2,1)} %copy.55), calls=%async_computation.1 | async-start | bytes 8388608 | tf_op jit(solution)/shard_map/all_to_all | solution.py:122
  623.8 53.7 %all-to-all-start.2 = ((bf16[16,128,1024]{2,1,0:T(8,128)(2,1)}), bf16[16,128,1024]{2,1,0:T(8,128)(2,1)}, u32[]{:S(2)}, u32[]{:S(2)}) async-start(bf16[16,128,1024]{2,1,0:T(8,128)(2,1)} %bitcast.147), calls=%async_computation.2 | async-start | bytes 8388608 | tf_op jit(solution)/shard_map/all_to_all | solution.py:249
  628.4 293.0 %all-reduce.16.cloned.1.call-start = ((), (), s32[]{:S(2)}) async-start(), calls=%async_computation.7 | async-start | bytes 12582912 | tf_op jit(solution)/shard_map/psum | solution.py:267
  628.5 9.1 copy-start.75
  680.4 12.7 copy-start.24
  681.0 14.1 %copy-start.74 = (bf16[2,1024,1024]{2,1,0:T(8,128)(2,1)S(1)}, bf16[2,1024,1024]{2,1,0:T(8,128)(2,1)}, u32[]{:S(2)}) copy-start(bf16[2,1024,1024]{2,1,0:T(8,128)(2,1)} %param.38) | copy-start | bytes 12582916
  930.0 53.8 %all-to-all-start.3 = ((bf16[2,1024,1024]{2,0,1:T(2,128)(2,1)}), bf16[2,1024,1024]{2,0,1:T(2,128)(2,1)}, u32[]{:S(2)}, u32[]{:S(2)}) async-start(bf16[2,1024,1024]{2,0,1:T(2,128)(2,1)} %copy.58), calls=%async_computation.3 | async-start | bytes 8388608 | tf_op jit(solution)/shard_map/all_to_all | solution.py:128
  934.7 211.2 %all-reduce.12.cloned.1.call-start = ((), (), s32[]{:S(2)}) async-start(), calls=%async_computation.5 | async-start | bytes 4194304 | tf_op jit(solution)/shard_map/psum | solution.py:293
  990.9 9.8 copy-start.49
  990.9 9.8 copy-start.51
  990.9 9.8 copy-start.54
  1000.7 7.7 copy-start.13
  1000.7 8.3 copy-start.21
  1062.5 192.2 %all-reduce.14.cloned.1.call-start = ((), (), s32[]{:S(2)}) async-start(), calls=%async_computation.6 | async-start | bytes 12582912 | tf_op jit(solution)/shard_map/psum | solution.py:315
  1077.8 13.7 %copy-start.23 = (bf16[2,8,128,1024]{3,2,1,0:T(8,128)(2,1)S(1)}, bf16[2,8,128,1024]{3,2,1,0:T(8,128)(2,1)}, u32[]{:S(2)}) copy-start(bf16[2,8,128,1024]{3,2,1,0:T(8,128)(2,1)} %copy-done.22) | copy-start | bytes 12582916
  1077.9 13.6 %copy-start.83 = (bf16[2,1024,1024]{2,1,0:T(8,128)(2,1)S(1)}, bf16[2,1024,1024]{2,1,0:T(8,128)(2,1)}, u32[]{:S(2)}) copy-start(bf16[2,1024,1024]{2,1,0:T(8,128)(2,1)} %copy-done.82) | copy-start | bytes 12582916
  1098.4 52.2 %copy-start.62 = (f32[1024]{0:T(1024)S(1)}, f32[1024]{0:T(1024)}, u32[]{:S(2)}) copy-start(f32[1024]{0:T(1024)} %copy-done.61) | copy-start | bytes 12292
  1147.9 35.8 %copy-start.60 = (f32[1024]{0:T(1024)S(1)}, f32[1024]{0:T(1024)}, u32[]{:S(2)}) copy-start(f32[1024]{0:T(1024)} %copy-done.59) | copy-start | bytes 12292
  (81 other events, 278.3 us)
Sparse Core Ops, SparseCore 0:
  45.9 157.6 all-reduce.9
  301.6 220.0 all-reduce.17
  701.5 219.9 all-reduce.15
  1062.6 83.2 all-reduce.11
  1150.5 104.1 all-reduce.13
where the time goes:
time: 1280 us; the launch traced here: 1270 us
  waiting for transfers between devices  869 us (68%)
  matrix products  142 us (11%)
  local copies, waits for them, and re-layouts  119 us (9%)
  other arithmetic  69.5 us (5%)
  blocking collectives  26.6 us (2%)
  starting transfers between devices  19.2 us (2%)
  between operations  14.9 us (1%)
    psum x1, waiting for transfers between devices, local(): lax.psum(dense_part.astype(jnp.bfloat16), 'tensor').astype(jnp.float32)  220 us
    psum x1, waiting for transfers between devices, local(): lax.psum(arrived_grad.astype(jnp.bfloat16), 'tensor').astype(jnp.float32)  220 us
    psum x1, waiting for transfers between devices, local(): attn_full = lax.psum(attn_part, 'tensor')  153 us
    psum x1, waiting for transfers between devices, local(): lax.psum(project_in_grad.astype(jnp.bfloat16), 'expert').astype(jnp.float32)  65.5 us
    psum x1, waiting for transfers between devices, local(): lax.psum(normed_part.astype(jnp.bfloat16), 'tensor').astype(jnp.float32)  47.4 us
    all_to_all x1, waiting for transfers between devices, send_home(): lax.all_to_all(buffer.astype(jnp.bfloat16), 'expert', split_axis=1, conca...  44.4 us
    all_to_all x1, waiting for transfers between devices, send_grads_home(): lax.all_to_all(buffer.astype(jnp.bfloat16), 'expert', split_axis=1, conca...  44.2 us
    all_to_all x1, waiting for transfers between devices, local(): lax.all_to_all(to_slots(mid_low), 'expert', split_axis=0, concat_axis=1,...  38.5 us
  transfers between devices with their start and end apart: 9, of which 9 were waited for; matrix products, arithmetic and copies ran while one was open for 7% of the time, Pallas kernels for 0%

commit v1 on v0

--- a/solution.py
+++ b/solution.py
@@ -165,7 +165,11 @@
     values = projected[:, 2].reshape(row_count, head_count, HEAD_DIM)
     attended, log_total = attend_forward(queries, key_rows, values, block_rows)
     attn_part = jnp.dot(attended, project_out, preferred_element_type=jnp.float32)
-    attn_full = lax.psum(attn_part, "tensor")
+    attn_full = attn_part
+    for hop in (1, 2):
+        attn_full = attn_full + lax.ppermute(
+            attn_full, "tensor", [(dev, dev ^ hop) for dev in range(4)]
+        )
     residual = inputs + attn_full
     normed_mid, second_back = jax.vjp(layer_norm, residual, second_gain, second_shift)
     mid_low = normed_mid.astype(jnp.bfloat16)

time: 1280 us -> 1420 us (1.11)
  waiting for transfers between devices: 869 us -> 970 us
  local copies, waits for them, and re-layouts: 119 us -> 150 us
    ppermute x0 -> x2, waiting for transfers between devices: none -> 266 us  [local(): lax.ppermute(attn_full, 'tensor', [(dev, dev ^ hop) for dev in range(4)])]
    psum x1 -> x0, waiting for transfers between devices: 153 us -> none  [local(): attn_full = lax.psum(attn_part, 'tensor')]
    unnamed x149 -> x155, local copies, waits for them, and re-layouts: 18.8 us -> 33.1 us
    gather x2 -> x4, local copies, waits for them, and re-layouts: 19.5 us -> 30.2 us  [from_slots(): jnp.take(buffer.reshape(slot_total, buffer.shape[-1]), slot_place, axis=0...]
  transfers between devices with their start and end apart: 9 -> 10, of which waited for: 9 -> 10; matrix products, arithmetic and copies ran while one was open for 7% -> 7% of each run, Pallas kernels for 0% -> 0%
where the time goes in v1:
time: 1420 us; the launch traced here: 1410 us
  waiting for transfers between devices  970 us (68%)
  local copies, waits for them, and re-layouts  150 us (11%)
  matrix products  144 us (10%)
  other arithmetic  72.8 us (5%)
  blocking collectives  26.6 us (2%)
  starting transfers between devices  24.7 us (2%)
  between operations  15.2 us (1%)
    ppermute x2, waiting for transfers between devices, local(): lax.ppermute(attn_full, 'tensor', [(dev, dev ^ hop) for dev in range(4)])  266 us
    psum x1, waiting for transfers between devices, local(): lax.psum(dense_part.astype(jnp.bfloat16), 'tensor').astype(jnp.float32)  222 us
    psum x1, waiting for transfers between devices, local(): lax.psum(arrived_grad.astype(jnp.bfloat16), 'tensor').astype(jnp.float32)  220 us
    psum x1, waiting for transfers between devices, local(): lax.psum(project_in_grad.astype(jnp.bfloat16), 'expert').astype(jnp.float32)  61.1 us
    psum x1, waiting for transfers between devices, local(): lax.psum(normed_part.astype(jnp.bfloat16), 'tensor').astype(jnp.float32)  43.6 us
    all_to_all x1, waiting for transfers between devices, send_home(): lax.all_to_all(buffer.astype(jnp.bfloat16), 'expert', split_axis=1, conca...  41 us
    all_to_all x1, waiting for transfers between devices, send_grads_home(): lax.all_to_all(buffer.astype(jnp.bfloat16), 'expert', split_axis=1, conca...  40.5 us
    all_to_all x1, waiting for transfers between devices, local(): lax.all_to_all(to_slots(mid_low), 'expert', split_axis=0, concat_axis=1,...  38.4 us
  transfers between devices with their start and end apart: 10, of which 10 were waited for; matrix products, arithmetic and copies ran while one was open for 7% of the time, Pallas kernels for 0%

profile of v1, /device:TPU:0, one launch (start us, length us, event | category | flops | bytes accessed | tf_op | source)
XLA Modules:
  0.0 1413.3 jit_solution(18000278929201628739)
XLA Ops:
  20.0 23.0 %while.43 = (s32[]{:T(128)}, bf16[2,512,4,64]{1,3,2,0:T(8,128)(2,1)}, f32[2,4,512]{2,1,0:T(4,128)S(1)}, s32[2]{0:T(128)S(1)}, bf16[1024,4,64]{0,2,1:T(8,128)(2,1...) while((s32[]{:T(128)}, ...), condition=%wide.region_5.6_spmd, body=%wide.region_2.5_spmd.sunk | while | flops 562690560 | bytes 35197428 | solution.py:55
  50.1 90.6 %collective-permute-done = f32[1024,1024]{0,1:T(8,128)S(1)} collective-permute-done((f32[1024,1024]{0,1:T(8,128)S(1)}, f32[1024,1024]{0,1:T(8,128)S(1)}, u32[]{:S(2)}, u32[]{:S(2)}) %collective-permute-start) | collective-permute-done | bytes 4194336 | tf_op jit(solution)/shard_map/ppermute | solution.py:170
  151.0 175.5 %collective-permute-done.1 = f32[1024,1024]{0,1:T(8,128)} collective-permute-done((f32[1024,1024]{0,1:T(8,128)}, f32[1024,1024]{0,1:T(8,128)}, u32[]{:S(2)}, u32[]{:S(2)}) %collective-permute-start.1) | collective-permute-done | bytes 4194336 | tf_op jit(solution)/shard_map/ppermute | solution.py:170
  340.7 12.8 gather_fusion
  372.6 38.4 %all-to-all-done = bf16[16,128,1024]{2,1,0:T(8,128)(2,1)} async-done(((bf16[16,128,1024]{2,1,0:T(8,128)(2,1)}), bf16[16,128,1024]{2,1,0:T(8,128)(2,1)}, u32[]{:S(2)}, u32[]{:S(2)}) %all-to-all-start) | async-done | bytes 4194336 | tf_op jit(solution)/shard_map/all_to_all | solution.py:209
  430.8 222.2 %all-reduce.15.cloned.1.call-done = (bf16[1024,1024]{0,1:T(8,128)(2,1)}, bf16[2,1024,1024]{2,1,0:T(8,128)(2,1)}) async-done(((bf16[1024,1024]{0,1:T(8,128)(2,1)}, bf16[2,1024,1024]{2,1,0:T(8,128)(2,1)}), (bf16[1024,1024]{0,1:T(8,128)(2,1)}, bf16[2,1024,1024]{2,1,0:T(8,128)(2,1)})) %all-reduce.15.cloned.1.call-update) | async-done | bytes 6291472 | tf_op jit(solution)/shard_map/psum | solution.py:221
  653.0 8.5 copy.85
  674.3 41.0 %all-to-all-done.1 = bf16[2,1024,1024]{2,0,1:T(2,128)(2,1)} async-done(((bf16[2,1024,1024]{2,0,1:T(2,128)(2,1)}), bf16[2,1024,1024]{2,0,1:T(2,128)(2,1)}, u32[]{:S(2)}, u32[]{:S(2)}) %all-to-all-start.1) | async-done | bytes 4194336 | tf_op jit(solution)/shard_map/all_to_all | solution.py:122
  715.3 7.1 copy.86
  722.5 9.7 gather_fusion.1
  748.2 12.8 gather_fusion.2
  769.5 7.4 fusion.62
  782.0 36.5 %all-to-all-done.2 = bf16[16,128,1024]{2,1,0:T(8,128)(2,1)} async-done(((bf16[16,128,1024]{2,1,0:T(8,128)(2,1)}), bf16[16,128,1024]{2,1,0:T(8,128)(2,1)}, u32[]{:S(2)}, u32[]{:S(2)}) %all-to-all-start.2) | async-done | bytes 4194336 | tf_op jit(solution)/shard_map/all_to_all | solution.py:253
  822.0 12.1 fusion.43
  842.6 220.1 %all-reduce.13.cloned.1.call-done = (bf16[2,1024,1024]{2,1,0:T(8,128)(2,1)}, bf16[1024,1024]{0,1:T(8,128)(2,1)}) async-done(((bf16[2,1024,1024]{2,1,0:T(8,128)(2,1)}, bf16[1024,1024]{0,1:T(8,128)(2,1)}), (bf16[2,1024,1024]{2,1,0:T(8,128)(2,1)}, bf16[1024,1024]{0,1:T(8,128)(2,1)})) %all-reduce.13.cloned.1.call-update) | async-done | bytes 6291472 | tf_op jit(solution)/shard_map/psum | solution.py:271
  1062.7 8.5 copy.92
  1084.4 40.5 %all-to-all-done.3 = bf16[2,1024,1024]{2,0,1:T(2,128)(2,1)} async-done(((bf16[2,1024,1024]{2,0,1:T(2,128)(2,1)}), bf16[2,1024,1024]{2,0,1:T(2,128)(2,1)}, u32[]{:S(2)}, u32[]{:S(2)}) %all-to-all-start.3) | async-done | bytes 4194336 | tf_op jit(solution)/shard_map/all_to_all | solution.py:128
  1132.0 9.8 gather_fusion.3
  1147.2 7.3 multiply_reduce_fusion.1
  1163.0 31.3 %while.44 = (s32[]{:T(128)}, f32[1024,4,64]{0,2,1:T(8,128)S(1)}, f32[1024,4,64]{0,2,1:T(8,128)}, bf16[2,512,4,64]{1,3,2,0:T(8,128)(2,1)}, s32[2]{0:T(128)S(1)}, ...) while((s32[]{:T(128)}, f32[1024,4,64]{0,2,1:T(8,128)S(1)}, ...), condition=%wide.region_26.29_spmd.clone, body=%wide.region_24.28_spmd.clone.sunk | while | flops 1375599104 | bytes 87093672 | solution.py:102
  1219.1 13.7 fusion.97
  1243.7 43.6 %all-reduce.9.cloned.1.call-done = bf16[1024,1024]{0,1:T(8,128)(2,1)} async-done(((bf16[1024,1024]{0,1:T(8,128)(2,1)}), bf16[1024,1024]{0,1:T(8,128)(2,1)}) %all-reduce.9.cloned.1.call-update) | async-done | bytes 2097168 | tf_op jit(solution)/shard_map/psum | solution.py:297
  1294.6 26.6 %all-reduce = (bf16[1024]{0:T(1024)(128)(2,1)S(1)}, bf16[1024]{0:T(1024)(128)(2,1)S(1)}, bf16[1024]{0:T(1024)(128)(2,1)S(1)}, bf16[1024]{0:T(1024)(128)(2,1)S(1)...) all-reduce(bf16[1024]{0:T(1024)(128)(2,1)S(1)} %get-tuple-element.3, ...), channel_id=1, replica_groups=mesh['expert'=8,'tensor'=4] {'expert'}, use_global_device_ids=true, to_apply=%region_31.34 | all-reduce | flops 22528 | bytes 90112 | tf_op jit(solution)/shard_map/psum | solution.py:320
  1334.5 61.1 %all-reduce.11.cloned.1.call-done = (bf16[1024,3,256]{2,0,1:T(8,128)(2,1)}, bf16[256,1024]{1,0:T(8,128)(2,1)}, bf16[1024,1024]{1,0:T(8,128)(2,1)}, bf16[1024,1024]{1,0:T(8,128)(2,1)}) async-done(((bf16[1024,3,256]{2,0,1:T(8,128)(2,1)}, bf16[256,1024]{1,0:T(8,128)(2,1)}, bf16[1024,1024]{1,0:T(8,128)(2,1)}, bf16[1024,1024]{1,0:T(8,128)(2,1)}), (bf16[1024,3,256]{2,0,1:T(8,128)(2,1)}, ...) | async-done | bytes 6291472 | tf_op jit(solution)/shard_map/psum | solution.py:319
  (329 shorter events, 281.3 us)
Async XLA Ops:
  7.2 361.5 %copy-start = (bf16[1024,1024]{1,0:T(8,128)(2,1)S(1)}, bf16[1024,1024]{1,0:T(8,128)(2,1)}, u32[]{:S(2)}) copy-start(bf16[1024,1024]{1,0:T(8,128)(2,1)} %param.37) | copy-start | bytes 6291460
  7.2 9.6 copy-start.53
  7.2 9.6 copy-start.75
  47.0 99.4 %copy-start.50 = (s32[1024]{0:T(1024)S(1)}, s32[1024]{0:T(1024)}, u32[]{:S(2)}) copy-start(s32[1024]{0:T(1024)} %param.26) | copy-start | bytes 12292
  47.0 99.4 %copy-start.68 = (s32[1024]{0:T(1024)S(1)}, s32[1024]{0:T(1024)}, u32[]{:S(2)}) copy-start(s32[1024]{0:T(1024)} %param.27) | copy-start | bytes 12292
  47.0 93.7 %collective-permute-start = (f32[1024,1024]{0,1:T(8,128)S(1)}, f32[1024,1024]{0,1:T(8,128)S(1)}, u32[]{:S(2)}, u32[]{:S(2)}) collective-permute-start(f32[1024,1024]{0,1:T(8,128)S(1)} %fusion.104), channel_id=1, source_target_pairs={{0,1},{1,0},{2,3},{3,2},{4,5},{5,4},{6,7},{7,6},{8,9},{9,8},{10,11... | collective-permute-start | bytes 12582920 | tf_op jit(solution)/shard_map/ppermute | solution.py:170
  143.6 182.8 %collective-permute-start.1 = (f32[1024,1024]{0,1:T(8,128)}, f32[1024,1024]{0,1:T(8,128)}, u32[]{:S(2)}, u32[]{:S(2)}) collective-permute-start(f32[1024,1024]{0,1:T(8,128)} %add.258), channel_id=1, source_target_pairs={{0,2},{1,3},{2,0},{3,1},{4,6},{5,7},{6,4},{7,5},{8,10},{9,11},{10,... | collective-permute-start | bytes 12582920 | tf_op jit(solution)/shard_map/ppermute | solution.py:170
  332.7 8.0 copy-start.61
  357.3 53.7 %all-to-all-start = ((bf16[16,128,1024]{2,1,0:T(8,128)(2,1)}), bf16[16,128,1024]{2,1,0:T(8,128)(2,1)}, u32[]{:S(2)}, u32[]{:S(2)}) async-start(bf16[16,128,1024]{2,1,0:T(8,128)(2,1)} %bitcast.148), calls=%async_computation | async-start | bytes 8388608 | tf_op jit(solution)/shard_map/all_to_all | solution.py:209
  361.9 291.0 %all-reduce.15.cloned.1.call-start = ((), (), s32[]{:S(2)}) async-start(), calls=%async_computation.7 | async-start | bytes 12582912 | tf_op jit(solution)/shard_map/psum | solution.py:221
  661.5 53.9 %all-to-all-start.1 = ((bf16[2,1024,1024]{2,0,1:T(2,128)(2,1)}), bf16[2,1024,1024]{2,0,1:T(2,128)(2,1)}, u32[]{:S(2)}, u32[]{:S(2)}) async-start(bf16[2,1024,1024]{2,0,1:T(2,128)(2,1)} %copy.85), calls=%async_computation.1 | async-start | bytes 8388608 | tf_op jit(solution)/shard_map/all_to_all | solution.py:122
  764.8 53.7 %all-to-all-start.2 = ((bf16[16,128,1024]{2,1,0:T(8,128)(2,1)}), bf16[16,128,1024]{2,1,0:T(8,128)(2,1)}, u32[]{:S(2)}, u32[]{:S(2)}) async-start(bf16[16,128,1024]{2,1,0:T(8,128)(2,1)} %bitcast.147), calls=%async_computation.2 | async-start | bytes 8388608 | tf_op jit(solution)/shard_map/all_to_all | solution.py:253
  769.4 293.3 %all-reduce.13.cloned.1.call-start = ((), (), s32[]{:S(2)}) async-start(), calls=%async_computation.6 | async-start | bytes 12582912 | tf_op jit(solution)/shard_map/psum | solution.py:271
  769.5 8.8 copy-start.73
  821.4 12.7 copy-start.22
  822.0 14.1 copy-start.72
  1071.2 53.7 %all-to-all-start.3 = ((bf16[2,1024,1024]{2,0,1:T(2,128)(2,1)}), bf16[2,1024,1024]{2,0,1:T(2,128)(2,1)}, u32[]{:S(2)}, u32[]{:S(2)}) async-start(bf16[2,1024,1024]{2,0,1:T(2,128)(2,1)} %copy.92), calls=%async_computation.3 | async-start | bytes 8388608 | tf_op jit(solution)/shard_map/all_to_all | solution.py:128
  1075.8 211.5 %all-reduce.9.cloned.1.call-start = ((), (), s32[]{:S(2)}) async-start(), calls=%async_computation.4 | async-start | bytes 4194304 | tf_op jit(solution)/shard_map/psum | solution.py:297
  1147.2 8.3 copy-start.19
  1203.9 191.8 %all-reduce.11.cloned.1.call-start = ((), (), s32[]{:S(2)}) async-start(), calls=%async_computation.5 | async-start | bytes 12582912 | tf_op jit(solution)/shard_map/psum | solution.py:319
  1219.0 13.8 copy-start.21
  1219.0 13.8 copy-start.82
  1243.7 48.2 %copy-start.60 = (f32[1024]{0:T(1024)S(1)}, f32[1024]{0:T(1024)}, u32[]{:S(2)}) copy-start(f32[1024]{0:T(1024)} %copy-done.59) | copy-start | bytes 12292
  1289.3 34.3 %copy-start.58 = (f32[1024]{0:T(1024)S(1)}, f32[1024]{0:T(1024)}, u32[]{:S(2)}) copy-start(f32[1024]{0:T(1024)} %copy-done.57) | copy-start | bytes 12292
  (77 other events, 287.8 us)
Sparse Core Ops, SparseCore 0:
  430.9 222.0 all-reduce.14
  842.7 219.9 all-reduce.12
  1204.0 83.2 all-reduce.8
  1291.3 104.2 all-reduce.10
